TPU v7x, 256 devices: a whole 4x4x8 slice. The times are simulated.
256 devices in a mesh: depth: 32 (over z, x), tile: 8 (over y, core).
Axes of the slice: x: 4, y: 4, z: 8, core: 2. Of those that a mesh axis runs over, the one named last changes fastest.
Arguments:
- volume: bfloat16 [256, 512, 4096], P('depth', 'tile'), may hold values from -6 to 6
- shear: int32 [256], replicated, may hold values from -64 to 64, as said below
- footprint: int32 [32, 2], P('depth'), may hold values from 0 to 4096, as said below
Outputs:
- frame: float32 [4, 512, 4096], P(None, 'tile', 'depth')
Inputs may be any that keep to these rules, and one draw needn't show every extreme that they name: Offsets follow a linear tilt over the slices with small jitter; shear[0] and shear[255] are the two ends of the range, in either order. footprint[b, 0] < 1024 and footprint[b, 1] > 3072 for every brick.
All inputs are finite; a program needn't handle non-finite values.
Results may differ from a plain program's by a relative error of at most 0.00085.
Values may be sent and summed in bfloat16 or wider, within the bound.
A program may use at most 64 MiB of HBM per device.

v0:
```python
import jax
import jax.numpy as jnp
from jax import lax
from jax.sharding import PartitionSpec as P

NY = 4096
SMAX = 64


def extended_2(x, sides, width):
    edges = {}
    for axis, dim in sides:
        count, length = (lax.axis_size(axis), x.shape[dim])
        up = [(i, (i + 1) % count) for i in range(count - 1)]
        last = lax.slice_in_dim(x, length - width, length, axis=dim)
        leading = lax.slice_in_dim(x, 0, width, axis=dim)
        edges[dim] = (
            lax.ppermute(last, axis, up),
            lax.ppermute(leading, axis, [(b, a) for a, b in up]),
        )
    done = []
    for _, dim in sides:
        low, high = edges[dim]
        around = [(width, width) if d in done else (0, 0) for d in range(x.ndim)]
        x = jnp.concatenate([jnp.pad(low, around), x, jnp.pad(high, around)], axis=dim)
        done.append(dim)
    return x


def colour(cur, gx, gy, gz, offset, low, high, absorb):
    norm = jnp.sqrt(gx * gx + gy * gy + gz * gz + 1.0)
    shade = 0.3 + 0.7 * jnp.abs(0.48 * gx + 0.6 * gy + 0.64 * gz) / norm
    alpha = 1.0 - jnp.exp(-absorb * cur * cur)
    rgba = jnp.stack(
        [
            shade * jax.nn.sigmoid(1.2 * cur + 0.2) * alpha,
            shade * jax.nn.sigmoid(-0.8 * cur) * alpha,
            shade * jax.nn.sigmoid(0.5 * cur - 0.3) * alpha,
            alpha,
        ]
    )
    padded = jnp.pad(rgba, ((0, 0), (0, 0), (SMAX, SMAX)))
    moved = lax.dynamic_slice_in_dim(padded, SMAX - offset, NY, 2)
    column = jnp.arange(NY, dtype=jnp.int32)
    inside = ((column >= low) & (column < high)).astype(jnp.float32)
    return moved * inside


def shards(volume, shear, footprint):
    slices = volume.shape[0]
    rows = volume.shape[1]
    bricks = lax.axis_size("depth")
    total = slices * bricks
    absorb = 2.0 / total
    flip = shear[0] > shear[total - 1]
    me = lax.axis_index("depth")
    local_shear = lax.dynamic_slice_in_dim(shear, me * slices, slices, 0)
    extended = extended_2(volume, (("depth", 0), ("tile", 1)), 1)

    def slice_step(step, acc):
        local = jnp.where(flip, slices - 1 - step, step).astype(jnp.int32)
        block = lax.dynamic_slice_in_dim(extended, local, 3, 0).astype(jnp.float32)
        cur = block[1, 1:-1]
        gz = 0.5 * (block[2, 1:-1] - block[0, 1:-1])
        gx = 0.5 * (block[1, 2:] - block[1, :-2])
        cols = jnp.pad(cur, ((0, 0), (1, 1)))
        gy = 0.5 * (cols[:, 2:] - cols[:, :-2])
        placed = colour(
            cur, gx, gy, gz, local_shear[local], footprint[0, 0], footprint[0, 1], absorb
        )
        return acc + (1.0 - acc[3:4]) * placed

    acc = lax.fori_loop(0, slices, slice_step, jnp.zeros((4, rows, NY), jnp.float32))
    partial_value = acc.astype(jnp.bfloat16)
    pieces = lax.all_to_all(partial_value[None], "depth", split_axis=3, concat_axis=0, tiled=True)

    def brick_step(position, image):
        source = jnp.where(flip, bricks - 1 - position, position).astype(jnp.int32)
        piece = lax.dynamic_index_in_dim(pieces, source, 0, keepdims=False).astype(jnp.float32)
        return image + (1.0 - image[3:4]) * piece

    start = jnp.zeros(pieces.shape[1:], jnp.float32)
    return lax.fori_loop(0, bricks, brick_step, start)


def solution(mesh):
    placed = (P("depth", "tile", None), P(), P("depth", None))
    return jax.shard_map(
        shards, mesh=mesh, in_specs=placed, out_specs=P(None, "tile", "depth"), check_vma=False
    )
```

profile of v0, /device:TPU:1, one launch (start us, length us, event | category | flops | bytes accessed | tf_op | source)
XLA Modules:
  0.0 256.1 jit_solution(9280403989751274987)
XLA Ops:
  1.3 4.0 %collective-permute-start.1 = (bf16[1,64,4096]{2,1,0:T(8,128)(2,1)S(1)}, bf16[1,64,4096]{2,1,0:T(8,128)(2,1)S(1)}, u32[]{:S(2)}, u32[]{:S(2)}) collective-permute-start(bf16[1,64,4096]{2,1,0:T(8,128)(2,1)S(1)} %get-tuple-element.317), channel_id=1, source_target_pairs={{0,8},{8,16},{16,24},{24,32},{32,40},{40,48},{48,56},{56,64},{64,7... | collective-permute-start | bytes 1572872 | tf_op jit(solution)/shard_map/ppermute | solution.py:18
  8.0 4.0 %collective-permute-start = (bf16[8,1,4096]{2,1,0:T(2,128)(2,1)S(1)}, bf16[8,1,4096]{2,1,0:T(2,128)(2,1)S(1)}, u32[]{:S(2)}, u32[]{:S(2)}) collective-permute-start(bf16[8,1,4096]{2,1,0:T(2,128)(2,1)S(1)} %get-tuple-element.319), channel_id=1, source_target_pairs={{0,1},{1,2},{2,3},{3,4},{4,5},{5,6},{6,7},{8,9},{9,10},{10,11},{11... | collective-permute-start | bytes 196616 | tf_op jit(solution)/shard_map/ppermute | solution.py:18
  19.6 6.6 %fusion.30 = bf16[10,66,4096]{2,1,0:T(8,128)(2,1)} fusion(bf16[8,1,4096]{2,1,0:T(2,128)(2,1)S(1)} %collective-permute-done.3, bf16[8,1,4096]{2,1,0:T(2,128)(2,1)S(1)} %collective-permute-done, bf16[1,64,4096]{2,1,0:T(8,128)(2,1)S(1)} %collective-permute-done.2, bf16[8,64,4096]{2,1,0:T(8,128)(2,1)} %param.7, bf16[1,64,4096]{2,1,0:T(8,128)(2,1)S(1)} %collective-permute-done.1), kind=kLoop, calls=%fused_computation.57 | loop fusion | flops 37847040 | bytes 10780672 | tf_op jit(solution)/shard_map/concatenate | solution.py:25
  26.2 135.3 %while.30 = (s32[]{:T(128)}, f32[4,64,4096]{2,1,0:T(8,128)}, pred[]{:T(512)}, bf16[10,66,4096]{2,1,0:T(8,128)(2,1)}, s32[8]{0:T(128)S(1)}, /*index=5*/s32[1,2]{1...) while((s32[]{:T(128)}, f32[4,64,4096]{2,1,0:T(8,128)}, ...), condition=%wide.region_1.2_spmd.clone, body=%wide.region_0.1_spmd.clone.sunk | while | flops 30973964 | bytes 48940876 | solution.py:73
  35.9 3.9 %fusion.48 = f32[4,64,4096]{2,1,0:T(8,128)} fusion(s32[]{:T(128)S(6)} %select_n.74, f32[1,64,4096]{2,1,0:T(8,128)S(1)} %get-tuple-element.391, f32[1,64,4096]{2,1,0:T(8,128)S(1)} %get-tuple-element.392, f32[1,64,4096]{2,1,0:T(8,128)S(1)} %copy-done, f32[1,64,4096]{2,1,0:T(8,128)S(1)} %get-tuple-element.394, f32[4096]{0:T(1024)S(1)} %fusion.46, ...), kind=kLoop, calls=%fused_computation.10.clone.1 | loop fusion | flops 15728640 | bytes 13649408 | tf_op jit(solution)/shard_map/while/body/eval_jaxpr/add | solution.py:71
  47.1 2.6 broadcast_select_fusion.4
  51.7 5.5 %fusion.48 = f32[4,64,4096]{2,1,0:T(8,128)} fusion(s32[]{:T(128)S(6)} %select_n.74, f32[1,64,4096]{2,1,0:T(8,128)S(1)} %get-tuple-element.391, f32[1,64,4096]{2,1,0:T(8,128)S(1)} %get-tuple-element.392, f32[1,64,4096]{2,1,0:T(8,128)S(1)} %copy-done, f32[1,64,4096]{2,1,0:T(8,128)S(1)} %get-tuple-element.394, f32[4096]{0:T(1024)S(1)} %fusion.46, ...), kind=kLoop, calls=%fused_computation.10.clone.1 | loop fusion | flops 15728640 | bytes 13649408 | tf_op jit(solution)/shard_map/while/body/eval_jaxpr/add | solution.py:71
  64.5 2.6 broadcast_select_fusion.4
  69.1 5.5 %fusion.48 = f32[4,64,4096]{2,1,0:T(8,128)} fusion(s32[]{:T(128)S(6)} %select_n.74, f32[1,64,4096]{2,1,0:T(8,128)S(1)} %get-tuple-element.391, f32[1,64,4096]{2,1,0:T(8,128)S(1)} %get-tuple-element.392, f32[1,64,4096]{2,1,0:T(8,128)S(1)} %copy-done, f32[1,64,4096]{2,1,0:T(8,128)S(1)} %get-tuple-element.394, f32[4096]{0:T(1024)S(1)} %fusion.46, ...), kind=kLoop, calls=%fused_computation.10.clone.1 | loop fusion | flops 15728640 | bytes 13649408 | tf_op jit(solution)/shard_map/while/body/eval_jaxpr/add | solution.py:71
  81.9 2.6 broadcast_select_fusion.4
  86.5 5.5 %fusion.48 = f32[4,64,4096]{2,1,0:T(8,128)} fusion(s32[]{:T(128)S(6)} %select_n.74, f32[1,64,4096]{2,1,0:T(8,128)S(1)} %get-tuple-element.391, f32[1,64,4096]{2,1,0:T(8,128)S(1)} %get-tuple-element.392, f32[1,64,4096]{2,1,0:T(8,128)S(1)} %copy-done, f32[1,64,4096]{2,1,0:T(8,128)S(1)} %get-tuple-element.394, f32[4096]{0:T(1024)S(1)} %fusion.46, ...), kind=kLoop, calls=%fused_computation.10.clone.1 | loop fusion | flops 15728640 | bytes 13649408 | tf_op jit(solution)/shard_map/while/body/eval_jaxpr/add | solution.py:71
  103.9 5.5 %fusion.48 = f32[4,64,4096]{2,1,0:T(8,128)} fusion(s32[]{:T(128)S(6)} %select_n.74, f32[1,64,4096]{2,1,0:T(8,128)S(1)} %get-tuple-element.391, f32[1,64,4096]{2,1,0:T(8,128)S(1)} %get-tuple-element.392, f32[1,64,4096]{2,1,0:T(8,128)S(1)} %copy-done, f32[1,64,4096]{2,1,0:T(8,128)S(1)} %get-tuple-element.394, f32[4096]{0:T(1024)S(1)} %fusion.46, ...), kind=kLoop, calls=%fused_computation.10.clone.1 | loop fusion | flops 15728640 | bytes 13649408 | tf_op jit(solution)/shard_map/while/body/eval_jaxpr/add | solution.py:71
  116.7 2.6 broadcast_select_fusion.4
  121.3 5.5 %fusion.48 = f32[4,64,4096]{2,1,0:T(8,128)} fusion(s32[]{:T(128)S(6)} %select_n.74, f32[1,64,4096]{2,1,0:T(8,128)S(1)} %get-tuple-element.391, f32[1,64,4096]{2,1,0:T(8,128)S(1)} %get-tuple-element.392, f32[1,64,4096]{2,1,0:T(8,128)S(1)} %copy-done, f32[1,64,4096]{2,1,0:T(8,128)S(1)} %get-tuple-element.394, f32[4096]{0:T(1024)S(1)} %fusion.46, ...), kind=kLoop, calls=%fused_computation.10.clone.1 | loop fusion | flops 15728640 | bytes 13649408 | tf_op jit(solution)/shard_map/while/body/eval_jaxpr/add | solution.py:71
  138.7 5.5 %fusion.48 = f32[4,64,4096]{2,1,0:T(8,128)} fusion(s32[]{:T(128)S(6)} %select_n.74, f32[1,64,4096]{2,1,0:T(8,128)S(1)} %get-tuple-element.391, f32[1,64,4096]{2,1,0:T(8,128)S(1)} %get-tuple-element.392, f32[1,64,4096]{2,1,0:T(8,128)S(1)} %copy-done, f32[1,64,4096]{2,1,0:T(8,128)S(1)} %get-tuple-element.394, f32[4096]{0:T(1024)S(1)} %fusion.46, ...), kind=kLoop, calls=%fused_computation.10.clone.1 | loop fusion | flops 15728640 | bytes 13649408 | tf_op jit(solution)/shard_map/while/body/eval_jaxpr/add | solution.py:71
  156.1 5.5 %fusion.48 = f32[4,64,4096]{2,1,0:T(8,128)} fusion(s32[]{:T(128)S(6)} %select_n.74, f32[1,64,4096]{2,1,0:T(8,128)S(1)} %get-tuple-element.391, f32[1,64,4096]{2,1,0:T(8,128)S(1)} %get-tuple-element.392, f32[1,64,4096]{2,1,0:T(8,128)S(1)} %copy-done, f32[1,64,4096]{2,1,0:T(8,128)S(1)} %get-tuple-element.394, f32[4096]{0:T(1024)S(1)} %fusion.46, ...), kind=kLoop, calls=%fused_computation.10.clone.1 | loop fusion | flops 15728640 | bytes 13649408 | tf_op jit(solution)/shard_map/while/body/eval_jaxpr/add | solution.py:71
  164.0 4.7 %copy.10 = bf16[4,64,4096]{1,0,2:T(4,128)(2,1)} copy(bf16[4,64,4096]{2,1,0:T(8,128)(2,1)S(1)} %convert_element_type.55) | data formatting | bytes 4194304
  168.7 5.3 %bitcast_bitcast_fusion = bf16[4096,1,4,64]{3,2,1,0:T(4,128)(2,1)} fusion(bf16[4,64,4096]{1,0,2:T(4,128)(2,1)} %copy.10), kind=kLoop, calls=%fused_computation.63 | loop fusion | bytes 4194304
  174.0 8.6 %reshape.29 = bf16[32,2,16384]{2,1,0:T(2,128)(2,1)} reshape(bf16[4096,1,4,64]{3,2,1,0:T(4,128)(2,1)} %bitcast_bitcast_fusion) | data formatting | bytes 4194304
  182.6 13.0 %all-to-all-start = ((bf16[32,2,16384]{2,1,0:T(2,128)(2,1)}), bf16[32,2,16384]{2,1,0:T(2,128)(2,1)S(1)}, u32[]{:S(2)}, u32[]{:S(2)}) async-start(bf16[32,2,16384]{2,1,0:T(2,128)(2,1)} %reshape.29), calls=%async_computation | async-start | bytes 4194304 | tf_op jit(solution)/shard_map/all_to_all | solution.py:75
  195.7 46.8 %all-to-all-done = bf16[32,2,16384]{2,1,0:T(2,128)(2,1)S(1)} async-done(((bf16[32,2,16384]{2,1,0:T(2,128)(2,1)}), bf16[32,2,16384]{2,1,0:T(2,128)(2,1)S(1)}, u32[]{:S(2)}, u32[]{:S(2)}) %all-to-all-start) | async-done | bytes 2097184 | tf_op jit(solution)/shard_map/all_to_all | solution.py:75
  242.5 4.0 %reshape.30 = bf16[4096,1,4,64]{3,2,1,0:T(4,128)(2,1)} reshape(bf16[32,2,16384]{2,1,0:T(2,128)(2,1)S(1)} %all-to-all-done) | data formatting | bytes 4194304
  246.5 5.4 %copy.9 = bf16[1,4,64,32,128]{4,2,1,3,0:T(8,128)(2,1)S(1)} copy(bf16[1,4,64,32,128]{2,1,4,3,0:T(4,128)(2,1)} %bitcast.87) | data formatting | bytes 4194304 | tf_op jit(solution)/shard_map/all_to_all | solution.py:75
  251.9 3.5 %while.31 = (s32[]{:T(128)}, f32[4,64,128]{2,1,0:T(8,128)S(1)}, pred[]{:T(512)}, bf16[32,4,64,128]{3,2,1,0:T(8,128)(2,1)S(1)}, s32[]{:T(128)}, /*index=5*/s32[]{:T(128)}, s32[]{:T(128)}, s32[]{:T(128)}) while((s32[]{:T(128)}, f32[4,64,128]{2,1,0:T(8,128)S(1)}, pred[]{:T(512)}, bf16[32,4,64,128]{3,2,1,0:T(8,128)(2,1)S(1)}, ...), condition=%wide.region_3.4_spmd.clone, body=%wide.region_2.3_spmd.clone.sunk | while | flops 172040 | bytes 688287 | solution.py:83
  (197 shorter events, 87.2 us)
Async XLA Ops:
  1.3 17.4 %collective-permute-start.1 = (bf16[1,64,4096]{2,1,0:T(8,128)(2,1)S(1)}, bf16[1,64,4096]{2,1,0:T(8,128)(2,1)S(1)}, u32[]{:S(2)}, u32[]{:S(2)}) collective-permute-start(bf16[1,64,4096]{2,1,0:T(8,128)(2,1)S(1)} %get-tuple-element.317), channel_id=1, source_target_pairs={{0,8},{8,16},{16,24},{24,32},{32,40},{40,48},{48,56},{56,64},{64,7... | collective-permute-start | bytes 1572872 | tf_op jit(solution)/shard_map/ppermute | solution.py:18
  5.3 14.4 %collective-permute-start.2 = (bf16[1,64,4096]{2,1,0:T(8,128)(2,1)S(1)}, bf16[1,64,4096]{2,1,0:T(8,128)(2,1)S(1)}, u32[]{:S(2)}, u32[]{:S(2)}) collective-permute-start(bf16[1,64,4096]{2,1,0:T(8,128)(2,1)S(1)} %get-tuple-element.318), channel_id=1, source_target_pairs={{8,0},{16,8},{24,16},{32,24},{40,32},{48,40},{56,48},{64,56},{72,6... | collective-permute-start | bytes 1572872 | tf_op jit(solution)/shard_map/ppermute | solution.py:19
  8.0 9.4 %collective-permute-start = (bf16[8,1,4096]{2,1,0:T(2,128)(2,1)S(1)}, bf16[8,1,4096]{2,1,0:T(2,128)(2,1)S(1)}, u32[]{:S(2)}, u32[]{:S(2)}) collective-permute-start(bf16[8,1,4096]{2,1,0:T(2,128)(2,1)S(1)} %get-tuple-element.319), channel_id=1, source_target_pairs={{0,1},{1,2},{2,3},{3,4},{4,5},{5,6},{6,7},{8,9},{9,10},{10,11},{11... | collective-permute-start | bytes 196616 | tf_op jit(solution)/shard_map/ppermute | solution.py:18
  12.1 6.6 %collective-permute-start.3 = (bf16[8,1,4096]{2,1,0:T(2,128)(2,1)S(1)}, bf16[8,1,4096]{2,1,0:T(2,128)(2,1)S(1)}, u32[]{:S(2)}, u32[]{:S(2)}) collective-permute-start(bf16[8,1,4096]{2,1,0:T(2,128)(2,1)S(1)} %get-tuple-element.320), channel_id=1, source_target_pairs={{1,0},{2,1},{3,2},{4,3},{5,4},{6,5},{7,6},{9,8},{10,9},{11,10},{12... | collective-permute-start | bytes 196616 | tf_op jit(solution)/shard_map/ppermute | solution.py:19
  17.4 8.8 %copy-start.2 = (s32[1,2]{1,0:T(1,128)S(1)}, s32[1,2]{1,0:T(1,128)}, u32[]{:S(2)}) copy-start(s32[1,2]{1,0:T(1,128)} %param.9) | copy-start | bytes 28
  33.5 2.3 copy-start
  47.1 4.6 %copy-start = (f32[1,64,4096]{2,1,0:T(8,128)S(1)}, f32[1,64,4096]{2,1,0:T(8,128)}, u32[]{:S(2)}) copy-start(f32[1,64,4096]{2,1,0:T(8,128)} %get-tuple-element.393) | copy-start | bytes 3145732 | tf_op jit(solution)/shard_map/while
  64.5 4.6 %copy-start = (f32[1,64,4096]{2,1,0:T(8,128)S(1)}, f32[1,64,4096]{2,1,0:T(8,128)}, u32[]{:S(2)}) copy-start(f32[1,64,4096]{2,1,0:T(8,128)} %get-tuple-element.393) | copy-start | bytes 3145732 | tf_op jit(solution)/shard_map/while
  81.9 4.6 %copy-start = (f32[1,64,4096]{2,1,0:T(8,128)S(1)}, f32[1,64,4096]{2,1,0:T(8,128)}, u32[]{:S(2)}) copy-start(f32[1,64,4096]{2,1,0:T(8,128)} %get-tuple-element.393) | copy-start | bytes 3145732 | tf_op jit(solution)/shard_map/while
  99.3 4.6 %copy-start = (f32[1,64,4096]{2,1,0:T(8,128)S(1)}, f32[1,64,4096]{2,1,0:T(8,128)}, u32[]{:S(2)}) copy-start(f32[1,64,4096]{2,1,0:T(8,128)} %get-tuple-element.393) | copy-start | bytes 3145732 | tf_op jit(solution)/shard_map/while
  116.7 4.6 %copy-start = (f32[1,64,4096]{2,1,0:T(8,128)S(1)}, f32[1,64,4096]{2,1,0:T(8,128)}, u32[]{:S(2)}) copy-start(f32[1,64,4096]{2,1,0:T(8,128)} %get-tuple-element.393) | copy-start | bytes 3145732 | tf_op jit(solution)/shard_map/while
  134.1 4.6 %copy-start = (f32[1,64,4096]{2,1,0:T(8,128)S(1)}, f32[1,64,4096]{2,1,0:T(8,128)}, u32[]{:S(2)}) copy-start(f32[1,64,4096]{2,1,0:T(8,128)} %get-tuple-element.393) | copy-start | bytes 3145732 | tf_op jit(solution)/shard_map/while
  151.5 4.6 %copy-start = (f32[1,64,4096]{2,1,0:T(8,128)S(1)}, f32[1,64,4096]{2,1,0:T(8,128)}, u32[]{:S(2)}) copy-start(f32[1,64,4096]{2,1,0:T(8,128)} %get-tuple-element.393) | copy-start | bytes 3145732 | tf_op jit(solution)/shard_map/while
  182.6 59.9 %all-to-all-start = ((bf16[32,2,16384]{2,1,0:T(2,128)(2,1)}), bf16[32,2,16384]{2,1,0:T(2,128)(2,1)S(1)}, u32[]{:S(2)}, u32[]{:S(2)}) async-start(bf16[32,2,16384]{2,1,0:T(2,128)(2,1)} %reshape.29), calls=%async_computation | async-start | bytes 4194304 | tf_op jit(solution)/shard_map/all_to_all | solution.py:75
  255.4 0.7 copy-start.1
where the time goes:
time: 260 us; the launch traced here: 256 us
  other arithmetic  125 us (48%)
  waiting for transfers between devices  49 us (19%)
  local copies, waits for them, and re-layouts  43.5 us (17%)
  starting transfers between devices  24.3 us (9%)
  loops' own time  12.6 us (5%)
    all_to_all x1, waiting for transfers between devices, shards(): lax.all_to_all(partial_value[None], 'depth', split_axis=3, concat_axis=0,...  46.8 us
    add x8, other arithmetic, slice_step(): return acc + (1.0 - acc[3:4]) * placed  42.2 us
    another operation x16, other arithmetic, colour(): jnp.stack([shade * jax.nn.sigmoid(1.2 * cur + 0.2) * alpha, shade * jax.n...  26.1 us
    unnamed x8, local copies, waits for them, and re-layouts  23.3 us
    while x40, other arithmetic  18.6 us
    convert_element_type x8, other arithmetic, slice_step(): block = lax.dynamic_slice_in_dim(extended, local, 3, 0).astype(jnp.float32)  15 us
    all_to_all x1, starting transfers between devices, shards(): lax.all_to_all(partial_value[None], 'depth', split_axis=3, concat_axis=0,...  13 us
    another operation x1, loops' own time, shards(): lax.fori_loop(0, slices, slice_step, jnp.zeros((4, rows, NY), jnp.float32))  11 us
  transfers between devices with their start and end apart: 5, of which 3 were waited for; matrix products, arithmetic and copies ran while one was open for 1% of the time, Pallas kernels for 0%

commit v1 on v0

v1 whole, which is shorter than its diff:
```python
import functools
import math

import jax
import jax.numpy as jnp
from jax import lax
from jax.experimental import pallas as pl
from jax.experimental.pallas import tpu as pltpu
from jax.sharding import PartitionSpec as P

MESH = pl.DeviceIdType.MESH
LANES = 128
WIDE = 2 * LANES
HALO = 8
LAG = 2
TILE = 16


def kernel(
    groups,
    members,
    shear_ref,
    foot_ref,
    vol_ref,
    out_ref,
    slab,
    above,
    below,
    weights,
    fields,
    sent,
    got,
    staged,
    merged,
    load_sem,
    row_send,
    row_recv,
    halo_send,
    halo_recv,
    x_send,
    x_recv,
    z_send,
    z_recv,
):
    slices, rows, columns = vol_ref.shape
    bricks = groups * members
    total = slices * bricks
    tiles = lax.axis_size("tile")
    me, tile = lax.axis_index("depth"), lax.axis_index("tile")
    z, x = me // members, me % members
    span = members * LANES
    wide = members // 2
    tall = rows + 2 * HALO
    decay = -(2.0 / total) * math.log2(math.e)
    flip = shear_ref[0] > shear_ref[total - 1]

    def offset(k):
        half = groups // 2
        return half + k // 2 - (k % 2) * (2 * (k // 2) + 1)

    def owner(k):
        return (z + offset(k)) % groups

    following, leading = (me + 1) % bricks, (me + bricks - 1) % bricks
    lower, upper = (tile + 1) % tiles, (tile + tiles - 1) % tiles

    barrier = pltpu.get_barrier_semaphore()

    def greet(depth_id, tile_id):
        pl.semaphore_signal(
            barrier, inc=1, device_id=(depth_id, tile_id), device_id_type=MESH
        )

    for d in range(1, members):
        greet(z * members + (x + d) % members, tile)
    for d in range(1, groups):
        greet(((z + d) % groups) * members + x, tile)
    greet(following, tile)
    greet(leading, tile)
    greet(me, lower)
    greet(me, upper)

    load = pltpu.make_async_copy(
        vol_ref,
        slab.at[pl.ds(1, slices), pl.ds(0, rows), pl.ds(LANES, columns)],
        load_sem,
    )
    load.start()
    pl.semaphore_wait(barrier, members + groups + 2)

    def halo(k, up):
        peer = following if up else leading
        piece = (peer // members + offset(k)) % groups
        start = pl.multiple_of(piece * span, LANES)
        return pltpu.make_async_remote_copy(
            src_ref=vol_ref.at[slices - 1 if up else 0, :, pl.ds(start, span)],
            dst_ref=slab.at[
                0 if up else slices + 1,
                pl.ds(0, rows),
                pl.ds(pl.multiple_of(start + LANES, LANES), span),
            ],
            send_sem=halo_send.at[0 if up else 1, k],
            recv_sem=halo_recv.at[0 if up else 1, k],
            device_id=(peer, tile),
            device_id_type=MESH,
        )

    def row_halo(down):
        return pltpu.make_async_remote_copy(
            src_ref=vol_ref.at[:, pl.ds(rows - HALO if down else 0, HALO), :],
            dst_ref=above if down else below,
            send_sem=row_send.at[0 if down else 1],
            recv_sem=row_recv.at[0 if down else 1],
            device_id=(me, lower if down else upper),
            device_id_type=MESH,
        )

    row_halo(True).start()
    row_halo(False).start()

    def start_halo(k, carry):
        halo(k, True).start()
        halo(k, False).start()
        return carry

    lax.fori_loop(0, groups, start_halo, 0)

    slab[:, :, 0:LANES] = jnp.zeros((slices + 2, tall, LANES), slab.dtype)
    slab[:, :, pl.ds(LANES + columns, LANES)] = jnp.zeros(
        (slices + 2, tall, LANES), slab.dtype
    )

    def weigh(s, carry):
        shift = shear_ref[me * slices + s]
        lead = lax.broadcasted_iota(jnp.int32, (WIDE, WIDE), 0)
        lead = lead - lax.broadcasted_iota(jnp.int32, (WIDE, WIDE), 1)
        for part, base in ((0, LANES), (1, -LANES)):
            at = lead - (base - shift)
            weights[s, part] = jnp.where(at == 0, 1.0, 0.0).astype(weights.dtype)
            weights[s, 2 + part] = (
                jnp.where(at == 1, 1.0, jnp.where(at == -1, -1.0, 0.0))
            ).astype(weights.dtype)
        return carry

    lax.fori_loop(0, slices, weigh, 0)

    load.wait()
    row_halo(True).wait_recv()
    row_halo(False).wait_recv()

    def join_rows(s, carry):
        low = jnp.where(tile < tiles - 1, below[s].astype(jnp.float32), 0.0)
        high = jnp.where(tile > 0, above[s].astype(jnp.float32), 0.0)
        slab[1 + s, pl.ds(rows, 2 * HALO), pl.ds(LANES, columns)] = jnp.concatenate(
            [low, high], axis=0
        ).astype(slab.dtype)
        return carry

    lax.fori_loop(0, slices, join_rows, 0)

    def await_halo(k):
        halo(k, True).wait_recv()
        halo(k, False).wait_recv()
        start = pl.multiple_of(owner(k) * span + LANES, LANES)

        @pl.when(me == 0)
        def _():
            slab[0, pl.ds(0, rows), pl.ds(start, span)] = jnp.zeros(
                (rows, span), slab.dtype
            )

        @pl.when(me == bricks - 1)
        def _():
            slab[slices + 1, pl.ds(0, rows), pl.ds(start, span)] = jnp.zeros(
                (rows, span), slab.dtype
            )

    def shift_slice(s, start):
        def block(i, j, height):
            at = pl.multiple_of(start + j * WIDE, LANES)
            return slab[i, pl.ds(0, height), pl.ds(at, WIDE)]

        cur = [block(s + 1, j, tall) for j in range(wide + 1)]
        nxt = [block(s + 2, j, rows) for j in range(wide + 1)]
        prv = [block(s, j, rows) for j in range(wide + 1)]

        def through(blocks, which):
            low = jnp.concatenate([b for one in blocks for b in one[:-1]], axis=0)
            high = jnp.concatenate([b for one in blocks for b in one[1:]], axis=0)
            return jnp.dot(
                low, weights[s, which], preferred_element_type=jnp.float32
            ) + jnp.dot(
                high, weights[s, which + 1], preferred_element_type=jnp.float32
            )

        moved = through([cur, nxt, prv], 0)
        sloped = through([[b[:rows] for b in cur]], 2)
        for j in range(wide):
            strip = moved[j * tall : (j + 1) * tall]
            at = wide * tall + j * rows
            after = moved[at : at + rows]
            at = wide * (tall + rows) + j * rows
            before = moved[at : at + rows]
            down = pltpu.roll(strip, tall - 1, 0)[:rows]
            up = pltpu.roll(strip, 1, 0)[:rows]
            found = (
                strip[:rows],
                down - up,
                sloped[j * rows : (j + 1) * rows],
                after - before,
            )
            for q, value in enumerate(found):
                for h in range(2):
                    fields[q, s, 2 * j + h] = value[:, h * LANES : (h + 1) * LANES]

    def shade_tile(k, i):
        block, part = i // (rows // TILE), i % (rows // TILE)
        at = pl.ds(pl.multiple_of(part * TILE, TILE), TILE)
        shape = (TILE, LANES)
        left = jnp.ones(shape, jnp.float32)
        base = jnp.zeros(shape, jnp.float32)
        tint = [jnp.zeros(shape, jnp.float32)] * 3
        for step in range(slices):
            s = jnp.where(flip, slices - 1 - step, step)
            v = fields[0, s, block, at]
            dx = fields[1, s, block, at]
            dy = fields[2, s, block, at]
            dz = fields[3, s, block, at]
            facing = jnp.abs(
                (0.35 * 0.48) * dx + (0.35 * 0.6) * dy + (0.35 * 0.64) * dz
            )
            shade = 0.15 + facing * lax.rsqrt(dx * dx + dy * dy + dz * dz + 4.0)
            rest = left * jnp.exp2(decay * (v * v))
            weight = (left - rest) * shade
            left = rest
            base = base + weight
            turns = (
                jnp.tanh(0.6 * v + 0.1),
                jnp.tanh(-0.4 * v),
                jnp.tanh(0.25 * v - 0.15),
            )
            tint = [t + weight * turn for t, turn in zip(tint, turns)]
        first = (owner(k) * members + block) * LANES
        column = first + lax.broadcasted_iota(jnp.int32, shape, 1)
        inside = (column >= foot_ref[0, 0]) & (column < foot_ref[0, 1])
        for c, value in enumerate([base + t for t in tint] + [1.0 - left]):
            sent[k, block, c, at] = jnp.where(inside, value, 0.0).astype(sent.dtype)

    def exchange(k, d):
        peer = (x + d) % members
        return pltpu.make_async_remote_copy(
            src_ref=sent.at[k, peer],
            dst_ref=got.at[k, x],
            send_sem=x_send.at[k, d],
            recv_sem=x_recv.at[k, d],
            device_id=(z * members + peer, tile),
            device_id_type=MESH,
        )

    def hand_over(k):
        return pltpu.make_async_remote_copy(
            src_ref=staged.at[k],
            dst_ref=merged.at[z],
            send_sem=z_send.at[k],
            recv_sem=z_recv.at[k],
            device_id=(owner(k) * members + x, tile),
            device_id_type=MESH,
        )

    def merge(k, last):
        for d in range(1, members):
            exchange(k, d).wait_recv()
        got[k, x] = sent[k, x]

        def part(i, carry):
            at = pl.ds(pl.multiple_of(i * TILE, TILE), TILE)
            pieces = [
                [got[k, b, c, at].astype(jnp.float32) for c in range(4)]
                for b in range(members)
            ]
            for step in range(members):
                piece = [
                    jnp.where(flip, pieces[members - 1 - step][c], pieces[step][c])
                    for c in range(4)
                ]
                if step == 0:
                    colour, left = piece[:3], 1.0 - piece[3]
                else:
                    colour = [p + left * q for p, q in zip(colour, piece[:3])]
                    left = left * (1.0 - piece[3])
            for c, value in enumerate(colour + [left]):
                if last:
                    merged[z, c, at] = value
                else:
                    staged[k, c, at] = value
            return carry

        lax.fori_loop(0, rows // TILE, part, 0)
        if not last:
            hand_over(k).start()

    for k in range(2):
        await_halo(k)

    def advance(k, carry):
        @pl.when(k + 2 < groups)
        def _():
            await_halo(k + 2)

        start = owner(k) * span

        def one_slice(s, inner):
            shift_slice(s, start)
            return inner

        lax.fori_loop(0, slices, one_slice, 0)

        def one_tile(i, inner):
            shade_tile(k, i)
            return inner

        lax.fori_loop(0, members * (rows // TILE), one_tile, 0)
        for d in range(1, members):
            exchange(k, d).start()

        @pl.when(k >= LAG)
        def _():
            merge(k - LAG, False)

        return carry

    lax.fori_loop(0, groups, advance, 0)
    for k in range(groups - LAG, groups - 1):
        merge(k, False)
    merge(groups - 1, True)

    def arrive(k, carry):
        hand_over(k).wait_recv()
        return carry

    lax.fori_loop(0, groups - 1, arrive, 0)

    def finish(i, carry):
        at = pl.ds(pl.multiple_of(i * TILE, TILE), TILE)
        for step in range(groups):
            g = jnp.where(flip, groups - 1 - step, step)
            piece = [merged[g, c, at] for c in range(4)]
            if step == 0:
                colour, left = piece[:3], piece[3]
            else:
                colour = [p + left * q for p, q in zip(colour, piece[:3])]
                left = left * piece[3]
        for c, value in enumerate(colour + [1.0 - left]):
            out_ref[c, at] = value
        return carry

    lax.fori_loop(0, rows // TILE, finish, 0)

    row_halo(True).wait_send()
    row_halo(False).wait_send()

    def settle(k, carry):
        halo(k, True).wait_send()
        halo(k, False).wait_send()
        for d in range(1, members):
            exchange(k, d).wait_send()

        @pl.when(k < groups - 1)
        def _():
            hand_over(k).wait_send()

        return carry

    lax.fori_loop(0, groups, settle, 0)


def solution(mesh):
    members = 4
    groups = mesh.shape["depth"] // members

    def shards(volume, shear, footprint):
        slices, rows, columns = volume.shape
        tall = rows + 2 * HALO
        dma = pltpu.SemaphoreType.DMA
        return pl.pallas_call(
            functools.partial(kernel, groups, members),
            out_shape=jax.ShapeDtypeStruct((4, rows, LANES), jnp.float32),
            in_specs=[
                pl.BlockSpec(memory_space=pltpu.SMEM),
                pl.BlockSpec(memory_space=pltpu.SMEM),
                pl.BlockSpec(memory_space=pl.ANY),
            ],
            out_specs=pl.BlockSpec(memory_space=pltpu.VMEM),
            scratch_shapes=[
                pltpu.VMEM((slices + 2, tall, columns + 2 * LANES), jnp.bfloat16),
                pltpu.VMEM((slices, HALO, columns), jnp.bfloat16),
                pltpu.VMEM((slices, HALO, columns), jnp.bfloat16),
                pltpu.VMEM((slices, 4, WIDE, WIDE), jnp.bfloat16),
                pltpu.VMEM((4, slices, members, rows, LANES), jnp.float32),
                pltpu.VMEM((groups, members, 4, rows, LANES), jnp.bfloat16),
                pltpu.VMEM((groups, members, 4, rows, LANES), jnp.bfloat16),
                pltpu.VMEM((groups, 4, rows, LANES), jnp.float32),
                pltpu.VMEM((groups, 4, rows, LANES), jnp.float32),
                dma,
                dma((2,)),
                dma((2,)),
                dma((2, groups)),
                dma((2, groups)),
                dma((groups, members)),
                dma((groups, members)),
                dma((groups,)),
                dma((groups,)),
            ],
            compiler_params=pltpu.CompilerParams(
                collective_id=0,
                has_side_effects=True,
                vmem_limit_bytes=48 * 2**20,
            ),
        )(shear, footprint, volume)

    return jax.shard_map(
        shards,
        mesh=mesh,
        in_specs=(P("depth", "tile", None), P(), P("depth", None)),
        out_specs=P(None, "tile", "depth"),
        check_vma=False,
    )
```

time: 260 us -> 63.8 us (0.25); the launches traced: 256 us -> 63.7 us
  other arithmetic: 125 us -> 0 us
  Pallas kernels: 0 us -> 59.5 us
  waiting for transfers between devices: 49 us -> 0 us
  local copies, waits for them, and re-layouts: 43.5 us -> 4.18 us
  starting transfers between devices: 24.3 us -> 0 us
  loops' own time: 12.6 us -> 0 us
    pallas_call x0 -> x1, Pallas kernels: none -> 59.5 us  [shards(): pl.pallas_call(functools.partial(kernel, groups, members), out_shape=jax....]
    all_to_all x1 -> x0, waiting for transfers between devices: 46.8 us -> none  [shards(): lax.all_to_all(partial_value[None], 'depth', split_axis=3, concat_axis=0,...]
    add x40 -> x0, other arithmetic: 43.5 us -> none  [the longest x8 42.2 us: slice_step(): return acc + (1.0 - acc[3:4]) * placed]
    convert_element_type x17 -> x0, other arithmetic: 27.7 us -> none  [the longest x8 15 us: slice_step(): block = lax.dynamic_slice_in_dim(extended, local, 3, 0).astype(jnp.float32)]
    another operation x16 -> x0, other arithmetic: 26.1 us -> none  [colour(): jnp.stack([shade * jax.nn.sigmoid(1.2 * cur + 0.2) * alpha, shade * jax.n...]
    unnamed x8 -> x7, local copies, waits for them, and re-layouts: 23.3 us -> 4.18 us
    while x40 -> x0, other arithmetic: 18.6 us -> none
    all_to_all x1 -> x0, starting transfers between devices: 13 us -> none  [shards(): lax.all_to_all(partial_value[None], 'depth', split_axis=3, concat_axis=0,...]
  transfers between devices with their start and end apart: 5 -> 0, of which waited for: 3 -> 0; matrix products, arithmetic and copies ran while one was open for 1% -> 0% of each run, Pallas kernels for 0% -> 0%
where the time goes in v1:
time: 63.8 us; the launch traced here: 63.7 us
  Pallas kernels  59.5 us (93%)
  local copies, waits for them, and re-layouts  4.18 us (7%)
    pallas_call x1, Pallas kernels, shards(): pl.pallas_call(functools.partial(kernel, groups, members), out_shape=jax....  59.5 us
    unnamed x7, local copies, waits for them, and re-layouts  4.18 us

profile of v1, /device:TPU:1, one launch (start us, length us, event | category | flops | bytes accessed | tf_op | source)
XLA Modules:
  0.0 63.7 jit_solution(12843244676685968180)
XLA Ops:
  0.0 0.0 copy-start
  0.0 2.2 %copy-done = bf16[8,64,4096]{2,1,0:T(8,128)(2,1)S(1)} copy-done((bf16[8,64,4096]{2,1,0:T(8,128)(2,1)S(1)}, bf16[8,64,4096]{2,1,0:T(8,128)(2,1)}, u32[]{:S(2)}) %copy-start) | copy-done | bytes 4194328
  2.2 0.0 copy-start.1
  2.2 0.7 %copy-done.1 = s32[256]{0:T(256)S(1)} copy-done((s32[256]{0:T(256)S(1)}, s32[256]{0:T(256)}, u32[]{:S(2)}) %copy-start.1) | copy-done | bytes 1048
  2.9 0.0 copy-start.2
  2.9 0.7 %copy-done.2 = s32[1,2]{1,0:T(1,128)S(1)} copy-done((s32[1,2]{1,0:T(1,128)S(1)}, s32[1,2]{1,0:T(1,128)}, u32[]{:S(2)}) %copy-start.2) | copy-done | bytes 32
  3.5 59.5 %shard_map.37 = f32[4,64,128]{2,1,0:T(8,128)S(1)} custom-call(s32[256]{0:T(256)S(1)} %copy-done.1, s32[1,2]{1,0:T(1,128)S(1)} %copy-done.2, bf16[8,64,4096]{2,1,0:T(8,128)(2,1)S(1)} %copy-done), custom_call_target="tpu_custom_call" | custom-call | tf_op jit(solution)/shard_map/pallas_call | solution.py:385
  63.0 0.7 %copy.5 = f32[4,64,128]{2,1,0:T(8,128)} copy(f32[4,64,128]{2,1,0:T(8,128)S(1)} %shard_map.37) | data formatting | bytes 262144
Async XLA Ops:
  0.0 2.2 %copy-start = (bf16[8,64,4096]{2,1,0:T(8,128)(2,1)S(1)}, bf16[8,64,4096]{2,1,0:T(8,128)(2,1)}, u32[]{:S(2)}) copy-start(bf16[8,64,4096]{2,1,0:T(8,128)(2,1)} %vol_ref.1) | copy-start | bytes 12582916
  2.2 0.7 %copy-start.1 = (s32[256]{0:T(256)S(1)}, s32[256]{0:T(256)}, u32[]{:S(2)}) copy-start(s32[256]{0:T(256)} %shear_ref.1) | copy-start | bytes 3076
  2.9 0.7 %copy-start.2 = (s32[1,2]{1,0:T(1,128)S(1)}, s32[1,2]{1,0:T(1,128)}, u32[]{:S(2)}) copy-start(s32[1,2]{1,0:T(1,128)} %foot_ref.1) | copy-start | bytes 28

commit v2 on v1

--- a/solution.py
+++ b/solution.py
@@ -19,10 +19,12 @@
 def kernel(
     groups,
     members,
+    shear_hbm,
+    foot_hbm,
+    vol_ref,
+    out_ref,
     shear_ref,
     foot_ref,
-    vol_ref,
-    out_ref,
     slab,
     above,
     below,
@@ -33,6 +35,7 @@
     staged,
     merged,
     load_sem,
+    table_sem,
     row_send,
     row_recv,
     halo_send,
@@ -52,7 +55,6 @@
     wide = members // 2
     tall = rows + 2 * HALO
     decay = -(2.0 / total) * math.log2(math.e)
-    flip = shear_ref[0] > shear_ref[total - 1]
 
     def offset(k):
         half = groups // 2
@@ -85,6 +87,12 @@
         slab.at[pl.ds(1, slices), pl.ds(0, rows), pl.ds(LANES, columns)],
         load_sem,
     )
+    tables = [
+        pltpu.make_async_copy(shear_hbm, shear_ref, table_sem.at[0]),
+        pltpu.make_async_copy(foot_hbm, foot_ref, table_sem.at[1]),
+    ]
+    for table in tables:
+        table.start()
     load.start()
     pl.semaphore_wait(barrier, members + groups + 2)
 
@@ -130,15 +138,20 @@
         (slices + 2, tall, LANES), slab.dtype
     )
 
+    for table in tables:
+        table.wait()
+    flip = shear_ref[0] > shear_ref[total - 1]
+
     def weigh(s, carry):
         shift = shear_ref[me * slices + s]
         lead = lax.broadcasted_iota(jnp.int32, (WIDE, WIDE), 0)
         lead = lead - lax.broadcasted_iota(jnp.int32, (WIDE, WIDE), 1)
         for part, base in ((0, LANES), (1, -LANES)):
             at = lead - (base - shift)
-            weights[s, part] = jnp.where(at == 0, 1.0, 0.0).astype(weights.dtype)
-            weights[s, 2 + part] = (
-                jnp.where(at == 1, 1.0, jnp.where(at == -1, -1.0, 0.0))
+            rows_at = pl.ds(part * WIDE, WIDE)
+            weights[s, 0, rows_at] = jnp.where(at == 0, 1.0, 0.0).astype(weights.dtype)
+            weights[s, 1, rows_at] = jnp.where(
+                at == 1, 1.0, jnp.where(at == -1, -1.0, 0.0)
             ).astype(weights.dtype)
         return carry
 
@@ -178,23 +191,21 @@
     def shift_slice(s, start):
         def block(i, j, height):
             at = pl.multiple_of(start + j * WIDE, LANES)
-            return slab[i, pl.ds(0, height), pl.ds(at, WIDE)]
-
-        cur = [block(s + 1, j, tall) for j in range(wide + 1)]
-        nxt = [block(s + 2, j, rows) for j in range(wide + 1)]
-        prv = [block(s, j, rows) for j in range(wide + 1)]
+            return slab[i, pl.ds(0, height), pl.ds(at, 2 * WIDE)]
+
+        cur = [block(s + 1, j, tall) for j in range(wide)]
+        nxt = [block(s + 2, j, rows) for j in range(wide)]
+        prv = [block(s, j, rows) for j in range(wide)]
 
         def through(blocks, which):
-            low = jnp.concatenate([b for one in blocks for b in one[:-1]], axis=0)
-            high = jnp.concatenate([b for one in blocks for b in one[1:]], axis=0)
             return jnp.dot(
-                low, weights[s, which], preferred_element_type=jnp.float32
-            ) + jnp.dot(
-                high, weights[s, which + 1], preferred_element_type=jnp.float32
-            )
-
-        moved = through([cur, nxt, prv], 0)
-        sloped = through([[b[:rows] for b in cur]], 2)
+                jnp.concatenate(blocks, axis=0),
+                weights[s, which],
+                preferred_element_type=jnp.float32,
+            )
+
+        moved = through(cur + nxt + prv, 0)
+        sloped = through([b[:rows] for b in cur], 1)
         for j in range(wide):
             strip = moved[j * tall : (j + 1) * tall]
             at = wide * tall + j * rows
@@ -313,13 +324,13 @@
             shift_slice(s, start)
             return inner
 
-        lax.fori_loop(0, slices, one_slice, 0)
+        lax.fori_loop(0, slices, one_slice, 0, unroll=8)
 
         def one_tile(i, inner):
             shade_tile(k, i)
             return inner
 
-        lax.fori_loop(0, members * (rows // TILE), one_tile, 0)
+        lax.fori_loop(0, members * (rows // TILE), one_tile, 0, unroll=2)
         for d in range(1, members):
             exchange(k, d).start()
 
@@ -386,22 +397,25 @@
             functools.partial(kernel, groups, members),
             out_shape=jax.ShapeDtypeStruct((4, rows, LANES), jnp.float32),
             in_specs=[
-                pl.BlockSpec(memory_space=pltpu.SMEM),
-                pl.BlockSpec(memory_space=pltpu.SMEM),
-                pl.BlockSpec(memory_space=pl.ANY),
+                pl.BlockSpec(memory_space=pltpu.HBM),
+                pl.BlockSpec(memory_space=pltpu.HBM),
+                pl.BlockSpec(memory_space=pltpu.HBM),
             ],
             out_specs=pl.BlockSpec(memory_space=pltpu.VMEM),
             scratch_shapes=[
+                pltpu.SMEM(shear.shape, jnp.int32),
+                pltpu.SMEM(footprint.shape, jnp.int32),
                 pltpu.VMEM((slices + 2, tall, columns + 2 * LANES), jnp.bfloat16),
                 pltpu.VMEM((slices, HALO, columns), jnp.bfloat16),
                 pltpu.VMEM((slices, HALO, columns), jnp.bfloat16),
-                pltpu.VMEM((slices, 4, WIDE, WIDE), jnp.bfloat16),
+                pltpu.VMEM((slices, 2, 2 * WIDE, WIDE), jnp.bfloat16),
                 pltpu.VMEM((4, slices, members, rows, LANES), jnp.float32),
                 pltpu.VMEM((groups, members, 4, rows, LANES), jnp.bfloat16),
                 pltpu.VMEM((groups, members, 4, rows, LANES), jnp.bfloat16),
                 pltpu.VMEM((groups, 4, rows, LANES), jnp.float32),
                 pltpu.VMEM((groups, 4, rows, LANES), jnp.float32),
                 dma,
+                dma((2,)),
                 dma((2,)),
                 dma((2,)),
                 dma((2, groups)),
@@ -416,7 +430,7 @@
                 has_side_effects=True,
                 vmem_limit_bytes=48 * 2**20,
             ),
-        )(shear, footprint, volume)
+        )(*(pltpu.with_memory_space_constraint(a, pltpu.HBM) for a in (shear, footprint, volume)))
 
     return jax.shard_map(
         shards,

time: 63.8 us -> 53.6 us (0.84)
  Pallas kernels: 59.5 us -> 52.9 us
  local copies, waits for them, and re-layouts: 4.18 us -> 0.66 us
    pallas_call x1, Pallas kernels: 59.5 us -> 52.9 us  [shards(): pl.pallas_call(functools.partial(kernel, groups, members), out_shape=jax....]
    unnamed x7 -> x1, local copies, waits for them, and re-layouts: 4.18 us -> 0.66 us
where the time goes in v2:
time: 53.6 us
  Pallas kernels  52.9 us (99%)
  local copies, waits for them, and re-layouts  0.66 us (1%)
    pallas_call x1, Pallas kernels, shards(): pl.pallas_call(functools.partial(kernel, groups, members), out_shape=jax....  52.9 us

profile of v2, /device:TPU:1, one launch (start us, length us, event | category | flops | bytes accessed | tf_op | source)
XLA Modules:
  0.0 53.6 jit_solution(6674359041358952262)
XLA Ops:
  0.0 52.9 %shard_map.37 = f32[4,64,128]{2,1,0:T(8,128)S(1)} custom-call(s32[256]{0:T(256)} %shear_hbm.1, s32[1,2]{1,0:T(1,128)} %foot_hbm.1, bf16[8,64,4096]{2,1,0:T(8,128)(2,1)} %vol_ref.1), custom_call_target="tpu_custom_call" | custom-call | tf_op jit(solution)/shard_map/pallas_call | solution.py:396
  52.9 0.7 %copy.5 = f32[4,64,128]{2,1,0:T(8,128)} copy(f32[4,64,128]{2,1,0:T(8,128)S(1)} %shard_map.37) | data formatting | bytes 262144

commit v3 on v2

--- a/solution.py
+++ b/solution.py
@@ -14,6 +14,8 @@
 HALO = 8
 LAG = 2
 TILE = 16
+UNROLL = 2
+SPREAD = 200.0
 
 
 def kernel(
@@ -29,7 +31,8 @@
     above,
     below,
     weights,
-    fields,
+    fields_even,
+    fields_odd,
     sent,
     got,
     staged,
@@ -96,39 +99,46 @@
     load.start()
     pl.semaphore_wait(barrier, members + groups + 2)
 
-    def halo(k, up):
+    def block_of(depth_id, u, h):
+        first = 2 * (depth_id // members) + groups
+        away = (u % 2) * (2 * u + 1) - u - 1
+        blocks = 2 * groups
+        return ((first + away + h + blocks) % blocks) * WIDE
+
+    def halo(u, h, up):
         peer = following if up else leading
-        piece = (peer // members + offset(k)) % groups
-        start = pl.multiple_of(piece * span, LANES)
+        start = pl.multiple_of(block_of(peer, u, h), LANES)
         return pltpu.make_async_remote_copy(
-            src_ref=vol_ref.at[slices - 1 if up else 0, :, pl.ds(start, span)],
+            src_ref=vol_ref.at[slices - 1 if up else 0, :, pl.ds(start, WIDE)],
             dst_ref=slab.at[
                 0 if up else slices + 1,
                 pl.ds(0, rows),
-                pl.ds(pl.multiple_of(start + LANES, LANES), span),
+                pl.ds(pl.multiple_of(start + LANES, LANES), WIDE),
             ],
-            send_sem=halo_send.at[0 if up else 1, k],
-            recv_sem=halo_recv.at[0 if up else 1, k],
+            send_sem=halo_send.at[0 if up else 1, u, h],
+            recv_sem=halo_recv.at[0 if up else 1, u, h],
             device_id=(peer, tile),
             device_id_type=MESH,
         )
 
-    def row_halo(down):
+    def row_halo(u, h, down):
+        at = pl.ds(pl.multiple_of(block_of(me, u, h), LANES), WIDE)
+        edge = pl.ds(rows - HALO if down else 0, HALO)
         return pltpu.make_async_remote_copy(
-            src_ref=vol_ref.at[:, pl.ds(rows - HALO if down else 0, HALO), :],
-            dst_ref=above if down else below,
-            send_sem=row_send.at[0 if down else 1],
-            recv_sem=row_recv.at[0 if down else 1],
+            src_ref=vol_ref.at[:, edge, at],
+            dst_ref=(above if down else below).at[:, :, at],
+            send_sem=row_send.at[0 if down else 1, u, h],
+            recv_sem=row_recv.at[0 if down else 1, u, h],
             device_id=(me, lower if down else upper),
             device_id_type=MESH,
         )
 
-    row_halo(True).start()
-    row_halo(False).start()
-
-    def start_halo(k, carry):
-        halo(k, True).start()
-        halo(k, False).start()
+    def start_halo(u, carry):
+        for h in range(2):
+            halo(u, h, True).start()
+            halo(u, h, False).start()
+            row_halo(u, h, True).start()
+            row_halo(u, h, False).start()
         return carry
 
     lax.fori_loop(0, groups, start_halo, 0)
@@ -158,37 +168,38 @@
     lax.fori_loop(0, slices, weigh, 0)
 
     load.wait()
-    row_halo(True).wait_recv()
-    row_halo(False).wait_recv()
-
-    def join_rows(s, carry):
-        low = jnp.where(tile < tiles - 1, below[s].astype(jnp.float32), 0.0)
-        high = jnp.where(tile > 0, above[s].astype(jnp.float32), 0.0)
-        slab[1 + s, pl.ds(rows, 2 * HALO), pl.ds(LANES, columns)] = jnp.concatenate(
-            [low, high], axis=0
-        ).astype(slab.dtype)
-        return carry
-
-    lax.fori_loop(0, slices, join_rows, 0)
-
-    def await_halo(k):
-        halo(k, True).wait_recv()
-        halo(k, False).wait_recv()
-        start = pl.multiple_of(owner(k) * span + LANES, LANES)
-
-        @pl.when(me == 0)
-        def _():
-            slab[0, pl.ds(0, rows), pl.ds(start, span)] = jnp.zeros(
-                (rows, span), slab.dtype
-            )
-
-        @pl.when(me == bricks - 1)
-        def _():
-            slab[slices + 1, pl.ds(0, rows), pl.ds(start, span)] = jnp.zeros(
-                (rows, span), slab.dtype
-            )
-
-    def shift_slice(s, start):
+
+    def await_rows(u):
+        for h in range(2):
+            row_halo(u, h, True).wait_recv()
+            row_halo(u, h, False).wait_recv()
+            start = pl.multiple_of(block_of(me, u, h), LANES)
+            at = pl.ds(start, WIDE)
+            low = jnp.where(tile < tiles - 1, below[:, :, at].astype(jnp.float32), 0.0)
+            high = jnp.where(tile > 0, above[:, :, at].astype(jnp.float32), 0.0)
+            at = pl.ds(pl.multiple_of(start + LANES, LANES), WIDE)
+            slab[pl.ds(1, slices), pl.ds(rows, 2 * HALO), at] = jnp.concatenate(
+                [low, high], axis=1
+            ).astype(slab.dtype)
+
+    def await_depth(u):
+        for h in range(2):
+            halo(u, h, True).wait_recv()
+            halo(u, h, False).wait_recv()
+            start = pl.multiple_of(block_of(me, u, h) + LANES, LANES)
+            at = pl.ds(start, WIDE)
+
+            @pl.when(me == 0)
+            def _():
+                slab[0, pl.ds(0, rows), at] = jnp.zeros((rows, WIDE), slab.dtype)
+
+            @pl.when(me == bricks - 1)
+            def _():
+                slab[slices + 1, pl.ds(0, rows), at] = jnp.zeros(
+                    (rows, WIDE), slab.dtype
+                )
+
+    def shift_slice(s, start, fields):
         def block(i, j, height):
             at = pl.multiple_of(start + j * WIDE, LANES)
             return slab[i, pl.ds(0, height), pl.ds(at, 2 * WIDE)]
@@ -224,7 +235,7 @@
                 for h in range(2):
                     fields[q, s, 2 * j + h] = value[:, h * LANES : (h + 1) * LANES]
 
-    def shade_tile(k, i):
+    def shade_tile(k, i, fields):
         block, part = i // (rows // TILE), i % (rows // TILE)
         at = pl.ds(pl.multiple_of(part * TILE, TILE), TILE)
         shape = (TILE, LANES)
@@ -278,6 +289,12 @@
             device_id_type=MESH,
         )
 
+    def spread(value):
+        return jnp.exp2(SPREAD * (value - 0.5))
+
+    def gather(code):
+        return jnp.log2(code) * (1.0 / SPREAD) + 0.5
+
     def merge(k, last):
         for d in range(1, members):
             exchange(k, d).wait_recv()
@@ -301,36 +318,37 @@
                     left = left * (1.0 - piece[3])
             for c, value in enumerate(colour + [left]):
                 if last:
-                    merged[z, c, at] = value
+                    merged[z, c, at] = spread(value).astype(merged.dtype)
                 else:
-                    staged[k, c, at] = value
+                    staged[k, c, at] = spread(value).astype(staged.dtype)
             return carry
 
         lax.fori_loop(0, rows // TILE, part, 0)
         if not last:
             hand_over(k).start()
 
-    for k in range(2):
-        await_halo(k)
-
-    def advance(k, carry):
-        @pl.when(k + 2 < groups)
-        def _():
-            await_halo(k + 2)
-
-        start = owner(k) * span
-
-        def one_slice(s, inner):
-            shift_slice(s, start)
-            return inner
-
-        lax.fori_loop(0, slices, one_slice, 0, unroll=8)
-
-        def one_tile(i, inner):
-            shade_tile(k, i)
-            return inner
-
-        lax.fori_loop(0, members * (rows // TILE), one_tile, 0, unroll=2)
+    each = members * (rows // TILE) // slices
+
+    def shade_only(k, fields):
+        def body(i, carry):
+            for t in range(each):
+                shade_tile(k, i * each + t, fields)
+            return carry
+
+        lax.fori_loop(0, slices, body, 0)
+
+    def shade_and_shift(k, fields, ahead):
+        start = owner(k + 1) * span
+
+        def body(i, carry):
+            shift_slice(i, start, ahead)
+            for t in range(each):
+                shade_tile(k, i * each + t, fields)
+            return carry
+
+        lax.fori_loop(0, slices, body, 0, unroll=UNROLL)
+
+    def pass_on(k):
         for d in range(1, members):
             exchange(k, d).start()
 
@@ -338,9 +356,37 @@
         def _():
             merge(k - LAG, False)
 
-        return carry
-
-    lax.fori_loop(0, groups, advance, 0)
+    await_rows(0)
+    await_rows(1)
+    first = owner(0) * span
+
+    def inner(s, carry):
+        shift_slice(s, first, fields_even)
+        return carry
+
+    lax.fori_loop(1, slices - 1, inner, 0, unroll=(slices - 2) // 2)
+    await_depth(0)
+    await_depth(1)
+    shift_slice(0, first, fields_even)
+    shift_slice(slices - 1, first, fields_even)
+
+    def advance(h, carry):
+        for part, fields, ahead in (
+            (0, fields_even, fields_odd),
+            (1, fields_odd, fields_even),
+        ):
+            k = 2 * h + part
+            await_rows(k + 2)
+            await_depth(k + 2)
+            shade_and_shift(k, fields, ahead)
+            pass_on(k)
+        return carry
+
+    lax.fori_loop(0, groups // 2 - 1, advance, 0)
+    shade_and_shift(groups - 2, fields_even, fields_odd)
+    pass_on(groups - 2)
+    shade_only(groups - 1, fields_odd)
+    pass_on(groups - 1)
     for k in range(groups - LAG, groups - 1):
         merge(k, False)
     merge(groups - 1, True)
@@ -355,7 +401,7 @@
         at = pl.ds(pl.multiple_of(i * TILE, TILE), TILE)
         for step in range(groups):
             g = jnp.where(flip, groups - 1 - step, step)
-            piece = [merged[g, c, at] for c in range(4)]
+            piece = [gather(merged[g, c, at].astype(jnp.float32)) for c in range(4)]
             if step == 0:
                 colour, left = piece[:3], piece[3]
             else:
@@ -367,12 +413,12 @@
 
     lax.fori_loop(0, rows // TILE, finish, 0)
 
-    row_halo(True).wait_send()
-    row_halo(False).wait_send()
-
     def settle(k, carry):
-        halo(k, True).wait_send()
-        halo(k, False).wait_send()
+        for h in range(2):
+            halo(k, h, True).wait_send()
+            halo(k, h, False).wait_send()
+            row_halo(k, h, True).wait_send()
+            row_halo(k, h, False).wait_send()
         for d in range(1, members):
             exchange(k, d).wait_send()
 
@@ -410,16 +456,17 @@
                 pltpu.VMEM((slices, HALO, columns), jnp.bfloat16),
                 pltpu.VMEM((slices, 2, 2 * WIDE, WIDE), jnp.bfloat16),
                 pltpu.VMEM((4, slices, members, rows, LANES), jnp.float32),
+                pltpu.VMEM((4, slices, members, rows, LANES), jnp.float32),
                 pltpu.VMEM((groups, members, 4, rows, LANES), jnp.bfloat16),
                 pltpu.VMEM((groups, members, 4, rows, LANES), jnp.bfloat16),
-                pltpu.VMEM((groups, 4, rows, LANES), jnp.float32),
-                pltpu.VMEM((groups, 4, rows, LANES), jnp.float32),
+                pltpu.VMEM((groups, 4, rows, LANES), jnp.bfloat16),
+                pltpu.VMEM((groups, 4, rows, LANES), jnp.bfloat16),
                 dma,
                 dma((2,)),
-                dma((2,)),
-                dma((2,)),
-                dma((2, groups)),
-                dma((2, groups)),
+                dma((2, groups, 2)),
+                dma((2, groups, 2)),
+                dma((2, groups, 2)),
+                dma((2, groups, 2)),
                 dma((groups, members)),
                 dma((groups, members)),
                 dma((groups,)),

time: 53.6 us -> 49.5 us (0.924)
  the two profiles are of different devices: /device:TPU:1 before, /device:TPU:8 now
where the time goes in v3:
time: 49.5 us; the launch traced here: 49.4 us
  Pallas kernels  48.8 us (99%)
  local copies, waits for them, and re-layouts  0.66 us (1%)
    pallas_call x1, Pallas kernels, shards(): pl.pallas_call(functools.partial(kernel, groups, members), out_shape=jax....  48.8 us

profile of v3, /device:TPU:8, one launch (start us, length us, event | category | flops | bytes accessed | tf_op | source)
XLA Modules:
  0.0 49.4 jit_solution(3160751895024695204)
XLA Ops:
  0.0 48.8 %shard_map.37 = f32[4,64,128]{2,1,0:T(8,128)S(1)} custom-call(s32[256]{0:T(256)} %shear_hbm.1, s32[1,2]{1,0:T(1,128)} %foot_hbm.1, bf16[8,64,4096]{2,1,0:T(8,128)(2,1)} %vol_ref.1), custom_call_target="tpu_custom_call" | custom-call | tf_op jit(solution)/shard_map/pallas_call | solution.py:442
  48.8 0.7 %copy.5 = f32[4,64,128]{2,1,0:T(8,128)} copy(f32[4,64,128]{2,1,0:T(8,128)S(1)} %shard_map.37) | data formatting | bytes 262144

commit v4 on v3

--- a/solution.py
+++ b/solution.py
@@ -12,10 +12,20 @@
 LANES = 128
 WIDE = 2 * LANES
 HALO = 8
-LAG = 2
+LAG = 3
 TILE = 16
 UNROLL = 2
 SPREAD = 200.0
+ORDERS = (
+    (4, 5, 6, 7, 1, 2, 3, 0),
+    (5, 6, 7, 4, 0, 2, 3, 1),
+    (6, 7, 4, 5, 0, 1, 3, 2),
+    (0, 1, 2, 7, 6, 5, 4, 3),
+    (0, 1, 2, 3, 5, 6, 7, 4),
+    (1, 2, 3, 0, 6, 7, 4, 5),
+    (2, 3, 0, 1, 7, 4, 5, 6),
+    (3, 0, 1, 2, 4, 5, 6, 7),
+)
 
 
 def kernel(
@@ -47,6 +57,7 @@
     x_recv,
     z_send,
     z_recv,
+    known,
 ):
     slices, rows, columns = vol_ref.shape
     bricks = groups * members
@@ -59,14 +70,21 @@
     tall = rows + 2 * HALO
     decay = -(2.0 / total) * math.log2(math.e)
 
-    def offset(k):
-        half = groups // 2
-        return half + k // 2 - (k % 2) * (2 * (k // 2) + 1)
+    half = groups // 2
+
+    code = 0
+    for plane, order in enumerate(ORDERS):
+        here = 1 - ((z - plane) * (z - plane) + groups * groups - 1) // (groups * groups)
+        code = code + here * sum(o * 8**k for k, o in enumerate(order))
 
     def owner(k):
-        return (z + offset(k)) % groups
-
-    following, leading = (me + 1) % bricks, (me + bricks - 1) % bricks
+        power = (1 + 7 * (k % 2)) * (1 + 63 * (k // 2 % 2)) * (1 + 4095 * (k // 4))
+        return code // power % 8
+
+    def upper_first(plane):
+        return (half - 2 - plane + groups) // groups
+
+    following, leading = me + 1, me - 1
     lower, upper = (tile + 1) % tiles, (tile + tiles - 1) % tiles
 
     barrier = pltpu.get_barrier_semaphore()
@@ -78,12 +96,38 @@
 
     for d in range(1, members):
         greet(z * members + (x + d) % members, tile)
-    for d in range(1, groups):
-        greet(((z + d) % groups) * members + x, tile)
-    greet(following, tile)
-    greet(leading, tile)
     greet(me, lower)
     greet(me, upper)
+
+    def towards(d, act):
+        pl.when(z + d < groups)(lambda: act(z + d, 0))
+        pl.when(z - d >= 0)(lambda: act(z - d, 1))
+
+    towards(1, lambda other, way: greet(other * members + x, tile))
+    pl.when(me < bricks - 1)(lambda: greet(following, tile))
+    pl.when(me > 0)(lambda: greet(leading, tile))
+
+    def some(left, count):
+        return (left + count - 1) // count
+
+    partners = members + 1 + some(me, bricks) + some(bricks - 1 - me, bricks)
+    partners = partners + some(z, groups) + some(groups - 1 - z, groups)
+
+    def tell(level):
+        def act(other, way):
+            pl.semaphore_signal(
+                known.at[level, way],
+                inc=1,
+                device_id=(other * members + x, tile),
+                device_id_type=MESH,
+            )
+
+        towards(2**level, act)
+
+    def hear(level):
+        towards(
+            2**level, lambda other, way: pl.semaphore_wait(known.at[level, 1 - way], 1)
+        )
 
     load = pltpu.make_async_copy(
         vol_ref,
@@ -97,17 +141,17 @@
     for table in tables:
         table.start()
     load.start()
-    pl.semaphore_wait(barrier, members + groups + 2)
-
-    def block_of(depth_id, u, h):
-        first = 2 * (depth_id // members) + groups
-        away = (u % 2) * (2 * u + 1) - u - 1
-        blocks = 2 * groups
-        return ((first + away + h + blocks) % blocks) * WIDE
-
-    def halo(u, h, up):
+    pl.semaphore_wait(barrier, partners)
+    tell(0)
+
+    blocks = columns // WIDE
+
+    def block_of(plane, u):
+        return u + upper_first(plane) * (blocks - 1 - 2 * u)
+
+    def halo(u, up):
         peer = following if up else leading
-        start = pl.multiple_of(block_of(peer, u, h), LANES)
+        start = pl.multiple_of(block_of(peer // members, u) * WIDE, LANES)
         return pltpu.make_async_remote_copy(
             src_ref=vol_ref.at[slices - 1 if up else 0, :, pl.ds(start, WIDE)],
             dst_ref=slab.at[
@@ -115,33 +159,32 @@
                 pl.ds(0, rows),
                 pl.ds(pl.multiple_of(start + LANES, LANES), WIDE),
             ],
-            send_sem=halo_send.at[0 if up else 1, u, h],
-            recv_sem=halo_recv.at[0 if up else 1, u, h],
+            send_sem=halo_send.at[0 if up else 1, u],
+            recv_sem=halo_recv.at[0 if up else 1, u],
             device_id=(peer, tile),
             device_id_type=MESH,
         )
 
-    def row_halo(u, h, down):
-        at = pl.ds(pl.multiple_of(block_of(me, u, h), LANES), WIDE)
+    def row_halo(u, down):
+        at = pl.ds(pl.multiple_of(block_of(z, u) * WIDE, LANES), WIDE)
         edge = pl.ds(rows - HALO if down else 0, HALO)
         return pltpu.make_async_remote_copy(
             src_ref=vol_ref.at[:, edge, at],
             dst_ref=(above if down else below).at[:, :, at],
-            send_sem=row_send.at[0 if down else 1, u, h],
-            recv_sem=row_recv.at[0 if down else 1, u, h],
+            send_sem=row_send.at[0 if down else 1, u],
+            recv_sem=row_recv.at[0 if down else 1, u],
             device_id=(me, lower if down else upper),
             device_id_type=MESH,
         )
 
     def start_halo(u, carry):
-        for h in range(2):
-            halo(u, h, True).start()
-            halo(u, h, False).start()
-            row_halo(u, h, True).start()
-            row_halo(u, h, False).start()
-        return carry
-
-    lax.fori_loop(0, groups, start_halo, 0)
+        pl.when(me < bricks - 1)(lambda: halo(u, True).start())
+        pl.when(me > 0)(lambda: halo(u, False).start())
+        row_halo(u, True).start()
+        row_halo(u, False).start()
+        return carry
+
+    lax.fori_loop(0, blocks, start_halo, 0)
 
     slab[:, :, 0:LANES] = jnp.zeros((slices + 2, tall, LANES), slab.dtype)
     slab[:, :, pl.ds(LANES + columns, LANES)] = jnp.zeros(
@@ -169,35 +212,34 @@
 
     load.wait()
 
-    def await_rows(u):
-        for h in range(2):
-            row_halo(u, h, True).wait_recv()
-            row_halo(u, h, False).wait_recv()
-            start = pl.multiple_of(block_of(me, u, h), LANES)
-            at = pl.ds(start, WIDE)
-            low = jnp.where(tile < tiles - 1, below[:, :, at].astype(jnp.float32), 0.0)
-            high = jnp.where(tile > 0, above[:, :, at].astype(jnp.float32), 0.0)
-            at = pl.ds(pl.multiple_of(start + LANES, LANES), WIDE)
-            slab[pl.ds(1, slices), pl.ds(rows, 2 * HALO), at] = jnp.concatenate(
-                [low, high], axis=1
-            ).astype(slab.dtype)
-
-    def await_depth(u):
-        for h in range(2):
-            halo(u, h, True).wait_recv()
-            halo(u, h, False).wait_recv()
-            start = pl.multiple_of(block_of(me, u, h) + LANES, LANES)
-            at = pl.ds(start, WIDE)
-
-            @pl.when(me == 0)
-            def _():
-                slab[0, pl.ds(0, rows), at] = jnp.zeros((rows, WIDE), slab.dtype)
-
-            @pl.when(me == bricks - 1)
-            def _():
-                slab[slices + 1, pl.ds(0, rows), at] = jnp.zeros(
-                    (rows, WIDE), slab.dtype
-                )
+    def await_rows(u, carry):
+        row_halo(u, True).wait_recv()
+        row_halo(u, False).wait_recv()
+        start = pl.multiple_of(block_of(z, u) * WIDE, LANES)
+        at = pl.ds(start, WIDE)
+        low = jnp.where(tile < tiles - 1, below[:, :, at].astype(jnp.float32), 0.0)
+        high = jnp.where(tile > 0, above[:, :, at].astype(jnp.float32), 0.0)
+        at = pl.ds(pl.multiple_of(start + LANES, LANES), WIDE)
+        slab[pl.ds(1, slices), pl.ds(rows, 2 * HALO), at] = jnp.concatenate(
+            [low, high], axis=1
+        ).astype(slab.dtype)
+        return carry
+
+    def await_depth(u, carry):
+        start = pl.multiple_of(block_of(z, u) * WIDE + LANES, LANES)
+        at = pl.ds(start, WIDE)
+        pl.when(me > 0)(lambda: halo(u, True).wait_recv())
+        pl.when(me < bricks - 1)(lambda: halo(u, False).wait_recv())
+
+        @pl.when(me == 0)
+        def _():
+            slab[0, pl.ds(0, rows), at] = jnp.zeros((rows, WIDE), slab.dtype)
+
+        @pl.when(me == bricks - 1)
+        def _():
+            slab[slices + 1, pl.ds(0, rows), at] = jnp.zeros((rows, WIDE), slab.dtype)
+
+        return carry
 
     def shift_slice(s, start, fields):
         def block(i, j, height):
@@ -284,18 +326,28 @@
             src_ref=staged.at[k],
             dst_ref=merged.at[z],
             send_sem=z_send.at[k],
-            recv_sem=z_recv.at[k],
+            recv_sem=z_recv.at[z],
             device_id=(owner(k) * members + x, tile),
             device_id_type=MESH,
         )
 
+    def handed(g):
+        return pltpu.make_async_remote_copy(
+            src_ref=staged.at[0],
+            dst_ref=merged.at[g],
+            send_sem=z_send.at[0],
+            recv_sem=z_recv.at[g],
+            device_id=(g * members + x, tile),
+            device_id_type=MESH,
+        )
+
     def spread(value):
         return jnp.exp2(SPREAD * (value - 0.5))
 
     def gather(code):
         return jnp.log2(code) * (1.0 / SPREAD) + 0.5
 
-    def merge(k, last):
+    def merge(k):
         for d in range(1, members):
             exchange(k, d).wait_recv()
         got[k, x] = sent[k, x]
@@ -317,15 +369,18 @@
                     colour = [p + left * q for p, q in zip(colour, piece[:3])]
                     left = left * (1.0 - piece[3])
             for c, value in enumerate(colour + [left]):
-                if last:
-                    merged[z, c, at] = spread(value).astype(merged.dtype)
-                else:
-                    staged[k, c, at] = spread(value).astype(staged.dtype)
+                staged[k, c, at] = spread(value).astype(staged.dtype)
             return carry
 
         lax.fori_loop(0, rows // TILE, part, 0)
-        if not last:
+
+        @pl.when(owner(k) != z)
+        def _():
             hand_over(k).start()
+
+        @pl.when(owner(k) == z)
+        def _():
+            merged[z] = staged[k]
 
     each = members * (rows // TILE) // slices
 
@@ -352,12 +407,16 @@
         for d in range(1, members):
             exchange(k, d).start()
 
+        pl.when(k == LAG)(lambda: hear(2))
+
         @pl.when(k >= LAG)
         def _():
-            merge(k - LAG, False)
-
-    await_rows(0)
-    await_rows(1)
+            merge(k - LAG)
+
+    hear(0)
+    tell(1)
+    soon = half * span // WIDE + 1
+    lax.fori_loop(0, soon, await_rows, 0)
     first = owner(0) * span
 
     def inner(s, carry):
@@ -365,8 +424,9 @@
         return carry
 
     lax.fori_loop(1, slices - 1, inner, 0, unroll=(slices - 2) // 2)
-    await_depth(0)
-    await_depth(1)
+    lax.fori_loop(0, soon, await_depth, 0)
+    hear(1)
+    tell(2)
     shift_slice(0, first, fields_even)
     shift_slice(slices - 1, first, fields_even)
 
@@ -376,8 +436,12 @@
             (1, fields_odd, fields_even),
         ):
             k = 2 * h + part
-            await_rows(k + 2)
-            await_depth(k + 2)
+
+            @pl.when(k == half - 2)
+            def _():
+                lax.fori_loop(soon, blocks, await_rows, 0)
+                lax.fori_loop(soon, blocks, await_depth, 0)
+
             shade_and_shift(k, fields, ahead)
             pass_on(k)
         return carry
@@ -387,15 +451,33 @@
     pass_on(groups - 2)
     shade_only(groups - 1, fields_odd)
     pass_on(groups - 1)
-    for k in range(groups - LAG, groups - 1):
-        merge(k, False)
-    merge(groups - 1, True)
-
-    def arrive(k, carry):
-        hand_over(k).wait_recv()
-        return carry
-
-    lax.fori_loop(0, groups - 1, arrive, 0)
+    def settle(u, carry):
+        pl.when(me < bricks - 1)(lambda: halo(u, True).wait_send())
+        pl.when(me > 0)(lambda: halo(u, False).wait_send())
+        row_halo(u, True).wait_send()
+        row_halo(u, False).wait_send()
+        return carry
+
+    def sent_on(k, carry):
+        for d in range(1, members):
+            exchange(k, d).wait_send()
+
+        @pl.when(owner(k) != z)
+        def _():
+            hand_over(k).wait_send()
+
+        return carry
+
+    lax.fori_loop(0, blocks, settle, 0)
+    lax.fori_loop(0, groups - LAG - 1, sent_on, 0)
+    for k in range(groups - LAG, groups):
+        merge(k)
+
+    def arrive(d, carry):
+        handed((z + d) % groups).wait_recv()
+        return carry
+
+    lax.fori_loop(1, groups, arrive, 0)
 
     def finish(i, carry):
         at = pl.ds(pl.multiple_of(i * TILE, TILE), TILE)
@@ -413,22 +495,7 @@
 
     lax.fori_loop(0, rows // TILE, finish, 0)
 
-    def settle(k, carry):
-        for h in range(2):
-            halo(k, h, True).wait_send()
-            halo(k, h, False).wait_send()
-            row_halo(k, h, True).wait_send()
-            row_halo(k, h, False).wait_send()
-        for d in range(1, members):
-            exchange(k, d).wait_send()
-
-        @pl.when(k < groups - 1)
-        def _():
-            hand_over(k).wait_send()
-
-        return carry
-
-    lax.fori_loop(0, groups, settle, 0)
+    lax.fori_loop(groups - LAG - 1, groups, sent_on, 0)
 
 
 def solution(mesh):
@@ -463,14 +530,15 @@
                 pltpu.VMEM((groups, 4, rows, LANES), jnp.bfloat16),
                 dma,
                 dma((2,)),
-                dma((2, groups, 2)),
-                dma((2, groups, 2)),
-                dma((2, groups, 2)),
-                dma((2, groups, 2)),
+                dma((2, columns // WIDE)),
+                dma((2, columns // WIDE)),
+                dma((2, columns // WIDE)),
+                dma((2, columns // WIDE)),
                 dma((groups, members)),
                 dma((groups, members)),
                 dma((groups,)),
                 dma((groups,)),
+                pltpu.SemaphoreType.REGULAR((3, 2)),
             ],
             compiler_params=pltpu.CompilerParams(
                 collective_id=0,

time: 49.5 us -> 46.4 us (0.937)
  the two profiles are of different devices: /device:TPU:8 before, /device:TPU:248 now
where the time goes in v4:
time: 46.4 us; the launch traced here: 46.3 us
  Pallas kernels  45.7 us (98%)
  local copies, waits for them, and re-layouts  0.66 us (1%)
    pallas_call x1, Pallas kernels, shards(): pl.pallas_call(functools.partial(kernel, groups, members), out_shape=jax....  45.7 us

profile of v4, /device:TPU:248, one launch (start us, length us, event | category | flops | bytes accessed | tf_op | source)
XLA Modules:
  0.0 46.3 jit_solution(12428108334933545982)
XLA Ops:
  0.0 45.7 %shard_map.37 = f32[4,64,128]{2,1,0:T(8,128)S(1)} custom-call(s32[256]{0:T(256)} %shear_hbm.1, s32[1,2]{1,0:T(1,128)} %foot_hbm.1, bf16[8,64,4096]{2,1,0:T(8,128)(2,1)} %vol_ref.1), custom_call_target="tpu_custom_call" | custom-call | tf_op jit(solution)/shard_map/pallas_call | solution.py:509
  45.7 0.7 %copy.5 = f32[4,64,128]{2,1,0:T(8,128)} copy(f32[4,64,128]{2,1,0:T(8,128)S(1)} %shard_map.37) | data formatting | bytes 262144

commit v5 on v4

--- a/solution.py
+++ b/solution.py
@@ -21,9 +21,9 @@
     (5, 6, 7, 4, 0, 2, 3, 1),
     (6, 7, 4, 5, 0, 1, 3, 2),
     (0, 1, 2, 7, 6, 5, 4, 3),
-    (0, 1, 2, 3, 5, 6, 7, 4),
-    (1, 2, 3, 0, 6, 7, 4, 5),
-    (2, 3, 0, 1, 7, 4, 5, 6),
+    (0, 1, 2, 3, 7, 6, 5, 4),
+    (1, 2, 3, 0, 7, 4, 6, 5),
+    (2, 3, 0, 1, 4, 7, 5, 6),
     (3, 0, 1, 2, 4, 5, 6, 7),
 )
 
@@ -404,7 +404,7 @@
         lax.fori_loop(0, slices, body, 0, unroll=UNROLL)
 
     def pass_on(k):
-        for d in range(1, members):
+        for d in (members // 2, 1, members - 1):
             exchange(k, d).start()
 
         pl.when(k == LAG)(lambda: hear(2))

time: 46.4 us -> 45.8 us (0.987)
  the two profiles are of different devices: /device:TPU:248 before, /device:TPU:127 now
where the time goes in v5:
time: 45.8 us; the launch traced here: 45.7 us
  Pallas kernels  45 us (98%)
  local copies, waits for them, and re-layouts  0.66 us (1%)
    pallas_call x1, Pallas kernels, shards(): pl.pallas_call(functools.partial(kernel, groups, members), out_shape=jax....  45 us

profile of v5, /device:TPU:127, one launch (start us, length us, event | category | flops | bytes accessed | tf_op | source)
XLA Modules:
  0.0 45.7 jit_solution(7827489371513846111)
XLA Ops:
  0.0 45.0 %shard_map.37 = f32[4,64,128]{2,1,0:T(8,128)S(1)} custom-call(s32[256]{0:T(256)} %shear_hbm.1, s32[1,2]{1,0:T(1,128)} %foot_hbm.1, bf16[8,64,4096]{2,1,0:T(8,128)(2,1)} %vol_ref.1), custom_call_target="tpu_custom_call" | custom-call | tf_op jit(solution)/shard_map/pallas_call | solution.py:509
  45.0 0.7 %copy.5 = f32[4,64,128]{2,1,0:T(8,128)} copy(f32[4,64,128]{2,1,0:T(8,128)S(1)} %shard_map.37) | data formatting | bytes 262144

commit v6 on v5

--- a/solution.py
+++ b/solution.py
@@ -178,8 +178,9 @@
         )
 
     def start_halo(u, carry):
+        pl.when((me > 0) & (x == 0))(lambda: halo(u, False).start())
         pl.when(me < bricks - 1)(lambda: halo(u, True).start())
-        pl.when(me > 0)(lambda: halo(u, False).start())
+        pl.when((me > 0) & (x > 0))(lambda: halo(u, False).start())
         row_halo(u, True).start()
         row_halo(u, False).start()
         return carry

time: 45.8 us -> 45.8 us (level)
  no operation moved by 1% of the time
where the time goes in v6:
time: 45.8 us; the launch traced here: 45.7 us
  Pallas kernels  45 us (98%)
  local copies, waits for them, and re-layouts  0.66 us (1%)
    pallas_call x1, Pallas kernels, shards(): pl.pallas_call(functools.partial(kernel, groups, members), out_shape=jax....  45 us

profile of v6, /device:TPU:127, one launch (start us, length us, event | category | flops | bytes accessed | tf_op | source)
XLA Modules:
  0.0 45.7 jit_solution(2005403448931709640)
XLA Ops:
  0.0 45.0 %shard_map.37 = f32[4,64,128]{2,1,0:T(8,128)S(1)} custom-call(s32[256]{0:T(256)} %shear_hbm.1, s32[1,2]{1,0:T(1,128)} %foot_hbm.1, bf16[8,64,4096]{2,1,0:T(8,128)(2,1)} %vol_ref.1), custom_call_target="tpu_custom_call" | custom-call | tf_op jit(solution)/shard_map/pallas_call | solution.py:510
  45.0 0.7 %copy.5 = f32[4,64,128]{2,1,0:T(8,128)} copy(f32[4,64,128]{2,1,0:T(8,128)S(1)} %shard_map.37) | data formatting | bytes 262144
